TPU v7x, 256 devices: a whole 4x4x8 slice. The times are simulated.
256 devices in a mesh: front: 8 (over x, core), grp: 32 (over y, z).
Axes of the slice: x: 4, y: 4, z: 8, core: 2. Of those that a mesh axis runs over, the one named last changes fastest.
Arguments:
- panel_block: bfloat16 [8, 4608, 1024], P('front', 'grp'), may hold values from -0.1796875 to 0.1796875
- trailing: float32 [8, 4608, 4608], P('front', 'grp')
- inverse: float32 [8, 1024, 1024], P('front')
- weights: float32 [8, 4608], P('front'), may hold values from -0.09375 to 0.09375
- live_size: int32 [8], P('front'), may hold values from 2304 to 4608, as said below
- column_source: int32 [8, 4608], P('front'), may hold values from 0 to 4607, each once within a row
- destination: int32 [8, 4608, 1], P('front', 'grp'), may hold values from 0 to 7; in each aligned block of 144 rows (0 to 143, 144 to 287, ..., all dimensions but the last counted through in order) at most 36 rows name the same one
- row_offset: int32 [8, 4608], P('front', 'grp'), may hold values from 0 to 143
Outputs:
- factor: float32 [8, 4608, 1024], P('front', 'grp')
- checksum: float32 [8, 4608], P('front', 'grp')
- ancestor: float32 [8, 4608, 4608], P('front', 'grp')
Inputs may be any that keep to these rules, and one draw needn't show every extreme that they name: `live_size`: each front's live size is 4608 minus a multiple of 576; one front is full. `destination`: among the 144 rows of one device at most 36 rows name the same ancestor front. `column_source`: each front's row is a permutation.
All inputs are finite; a program needn't handle non-finite values.
Results may differ from a plain program's by a relative error of at most 0.0003.
Values may be sent and summed in bfloat16 or wider, within the bound.
A program may use at most 128 MiB of HBM per device.

v0:
```python
import jax
import jax.numpy as jnp
from jax import lax
from jax.sharding import PartitionSpec as P

HIGHEST = lax.Precision.HIGHEST


def bf16_terms(x):
    high = lax.reduce_precision(x, 8, 7)
    rest = x - high
    middle = lax.reduce_precision(rest, 8, 7)
    low = rest - middle
    return [t.astype(jnp.bfloat16) for t in (high, middle, low)]


def on_device(
    panel_block, trailing, inverse, weights, live_size, column_source, destination, row_offset
):
    row_count = trailing.shape[1]
    col_count = trailing.shape[2]
    fronts = lax.axis_size("front")
    capacity = max(2, 2 * row_count // fronts)
    slots = fronts * capacity
    trail_rows = trailing[0]
    inverse_rows = inverse[0]
    live_count = live_size[0]
    panel_all = lax.all_gather(panel_block[0], "grp", axis=0, tiled=True)
    panel_f32 = panel_block[0].astype(jnp.float32)
    factor = jnp.dot(panel_f32, inverse_rows.T, precision=HIGHEST)
    twice = jnp.dot(factor, inverse_rows, precision=HIGHEST)
    rows = jnp.arange(row_count, dtype=jnp.int32)
    live_rows = lax.axis_index("grp") * row_count + rows < live_count
    dest_front = jnp.where(live_rows, destination[0, :, 0], -1)
    earlier = (dest_front[:, None] == dest_front[None, :]) & (rows[None, :] < rows[:, None])
    slot_index = jnp.sum(earlier.astype(jnp.int32), axis=1)
    flat_slot = jnp.where(live_rows, dest_front * capacity + slot_index, -1)
    place = flat_slot[None, :] == jnp.arange(slots, dtype=jnp.int32)[:, None]
    row_tags = jnp.sum(jnp.where(place, row_offset[0][None, :] + 1, 0), axis=1) - 1
    row_tags = row_tags.astype(jnp.float32).reshape(fronts, capacity)
    received_tags = lax.all_to_all(row_tags, "front", split_axis=0, concat_axis=0, tiled=True)
    targets = received_tags.reshape(slots).astype(jnp.int32)
    land = (targets[None, :] == rows[:, None]).astype(jnp.float32)
    source = column_source[0]
    keep = (source < live_count).astype(jnp.float32)
    trail_permuted = jnp.take(trail_rows, source, axis=1)
    kept_weights = jnp.take(weights[0], source) * keep
    update = sum(
        (
            lax.dot_general(
                term, panel_all, (((1,), (1,)), ((), ())), preferred_element_type=jnp.float32
            )
            for term in bf16_terms(twice)
        )
    )
    permuted = (trail_permuted - jnp.take(update, source, axis=1)) * keep[None, :]
    checksum = jnp.dot(permuted, kept_weights, precision=HIGHEST)
    bucket = jnp.dot(place.astype(jnp.float32), permuted, precision=HIGHEST)
    received = lax.all_to_all(
        bucket.reshape(fronts, capacity, col_count),
        "front",
        split_axis=0,
        concat_axis=0,
        tiled=True,
    )
    ancestor = jnp.dot(land, received.reshape(slots, col_count), precision=HIGHEST)
    return (factor[None], checksum[None], ancestor[None])


def solution(mesh):
    placed = (
        P("front", "grp", None),
        P("front", "grp", None),
        P("front", None, None),
        P("front", None),
        P("front"),
        P("front", None),
        P("front", "grp", None),
        P("front", "grp"),
    )
    return jax.shard_map(
        on_device,
        mesh=mesh,
        in_specs=placed,
        out_specs=(P("front", "grp", None), P("front", "grp"), P("front", "grp", None)),
        check_vma=False,
    )
```

profile of v0, /device:TPU:1, one launch (start us, length us, event | category | flops | bytes accessed | tf_op | source)
XLA Modules:
  0.0 257.4 jit_solution(17557925677657125797)
XLA Ops:
  7.2 0.0 copy-start
  7.2 0.0 copy-start.5
  7.2 0.0 all-gather.3.cloned.1.call-start
  7.2 0.7 all-gather.3.cloned.1.call-update
  8.6 0.7 fusion.28
  9.3 0.2 convert_reduce_fusion
  9.5 0.7 broadcast_add_fusion
  10.1 0.7 add_select_fusion
  10.8 0.1 select_reduce_fusion
  11.0 0.7 convert_element_type.46
  11.6 6.5 %all-to-all-start = ((f32[8,1,36]{2,1,0:T(1,128)}), f32[8,1,36]{2,1,0:T(1,128)S(1)}, u32[]{:S(2)}, u32[]{:S(2)}) async-start(f32[8,1,36]{2,1,0:T(1,128)} %convert_element_type.46), calls=%async_computation | async-start | bytes 8192 | tf_op jit(solution)/shard_map/all_to_all | solution.py:41
  18.1 5.1 %copy.15 = f32[1,144,4608]{1,2,0:T(8,128)} copy(f32[1,144,4608]{2,1,0:T(8,128)} %param.11) | data formatting | bytes 5308416 | tf_op args[1]
  23.2 0.0 copy-done.5
  23.3 0.0 copy-start.4
  23.3 14.1 %gather_fusion.1 = f32[4608,144]{1,0:T(8,128)} fusion(f32[144,4608]{0,1:T(8,128)} %bitcast.46, s32[5120]{0:T(1024)S(1)} %pad_clamp_fusion.1), kind=kCustom, calls=%fused_computation.clone | custom fusion | bytes 5326848 | tf_op jit(solution)/shard_map/jit(_take)/gather | solution.py:46
  37.4 0.0 copy-start.2
  37.4 0.1 fusion.27
  37.5 0.0 copy-done.4
  37.5 4.8 %fusion.15 = f32[144,1024]{1,0:T(8,128)S(1)} fusion(f32[1,1024,1024]{2,1,0:T(8,128)} %param.12, bf16[1,144,1024]{2,1,0:T(8,128)(2,1)S(1)} %copy-done.4), kind=kOutput, calls=%fused_computation.16 | convolution fusion | flops 1811939328 | bytes 5079040 | tf_op jit(solution)/shard_map/dot_general | solution.py:30
  42.3 0.0 copy-start.3
  42.3 0.8 copy-done.3
  43.1 0.0 copy-done.2
  43.1 2.6 fusion.13
  45.7 71.8 %all-gather.3.cloned.1.call-done = bf16[1,4608,1024]{2,1,0:T(8,128)(2,1)} async-done(((bf16[1,144,1024]{2,1,0:T(8,128)(2,1)}), bf16[1,4608,1024]{2,1,0:T(8,128)(2,1)}) %all-gather.3.cloned.1.call-update) | async-done | bytes 9437200 | tf_op jit(solution)/shard_map/all_gather | solution.py:28
  117.6 0.0 copy-start.1
  117.6 7.1 %fusion = f32[144,4608]{1,0:T(8,128)S(1)} fusion(bf16[1,4608,1024]{2,1,0:T(8,128)(2,1)} %all-gather.3.cloned.1.call-done, f32[144,1024]{1,0:T(8,128)S(1)} %fusion.13), kind=kOutput, calls=%fused_computation.3 | convolution fusion | flops 1359691776 | bytes 12681216 | tf_op jit(solution)/shard_map/dot_general | solution.py:50
  124.7 0.0 copy-done.1
  124.7 3.3 %fusion.2 = f32[144,4608]{1,0:T(8,128)S(1)} fusion(bf16[1,4608,1024]{2,1,0:T(8,128)(2,1)S(1)} %copy-done.1, f32[144,1024]{1,0:T(8,128)S(1)} %fusion.13), kind=kOutput, calls=%fused_computation.5 | convolution fusion | flops 1359544320 | bytes 12681216 | tf_op jit(solution)/shard_map/dot_general | solution.py:50
  127.9 3.3 %fusion.9 = f32[144,4608]{1,0:T(8,128)S(1)} fusion(f32[144,4608]{1,0:T(8,128)S(1)} %fusion, f32[144,4608]{1,0:T(8,128)S(1)} %fusion.2, bf16[1,4608,1024]{2,1,0:T(8,128)(2,1)S(1)} %copy-done.1, f32[144,1024]{1,0:T(8,128)S(1)} %fusion.13), kind=kOutput, calls=%fused_computation.11 | convolution fusion | flops 1360576512 | bytes 17989632 | tf_op jit(solution)/shard_map/dot_general | solution.py:50
  131.3 3.4 %copy.16 = f32[144,4608]{0,1:T(8,128)} copy(f32[144,4608]{1,0:T(8,128)S(1)} %fusion.9) | data formatting | bytes 5308416 | tf_op jit(solution)/shard_map/add | solution.py:48
  134.6 14.1 %gather_fusion.2 = f32[4608,144]{1,0:T(8,128)} fusion(f32[144,4608]{0,1:T(8,128)} %copy.16, s32[5120]{0:T(1024)S(1)} %pad_clamp_fusion.1), kind=kCustom, calls=%fused_computation.1.clone | custom fusion | bytes 5326848 | tf_op jit(solution)/shard_map/jit(_take)/gather | solution.py:56
  148.8 10.9 %fusion.22 = f32[288,4608]{1,0:T(8,128)} fusion(s32[144]{0:T(256)S(1)} %add_select_fusion, f32[4608,144]{1,0:T(8,128)} %gather_fusion.2, f32[4608,144]{1,0:T(8,128)} %gather_fusion.1, f32[4608]{0:T(1024)S(1)} %fusion.27, pred[4608]{0:T(1024)(128)(4,1)S(1)} %compare_and_fusion), kind=kOutput, calls=%fused_computation.31 | convolution fusion | flops 2295972864 | bytes 10640448 | tf_op jit(solution)/shard_map/dot_general | solution.py:58
  159.7 5.6 %reshape.109 = f32[8,36,4608]{2,1,0:T(8,128)} reshape(f32[288,4608]{1,0:T(8,128)} %fusion.22) | data formatting | bytes 10616832 | tf_op jit(solution)/shard_map/reshape | solution.py:60
  165.3 0.0 all-to-all-done
  165.3 5.7 %all-to-all-start.1 = ((f32[8,36,4608]{2,1,0:T(8,128)}), f32[8,36,4608]{2,1,0:T(8,128)}, u32[]{:S(2)}, u32[]{:S(2)}) async-start(f32[8,36,4608]{2,1,0:T(8,128)} %reshape.109), calls=%async_computation.1 | async-start | bytes 11796480 | tf_op jit(solution)/shard_map/all_to_all | solution.py:59
  171.0 0.0 copy-done
  171.0 0.1 fusion.26
  171.1 24.1 %gather_fusion = f32[4608]{0:T(1024)S(1)} fusion(f32[4608]{0:T(1024)S(1)} %reduce.2, s32[5120]{0:T(1024)S(1)} %pad_clamp_fusion), kind=kCustom, calls=%fused_computation.2 | custom fusion | bytes 55296 | tf_op jit(solution)/shard_map/jit(_take)/gather | solution.py:47
  195.2 0.1 convert_element_type.48
  195.3 7.5 %fusion.30 = f32[1,144]{1,0:T(1,128)} fusion(f32[4608,1]{0,1:T(1,128)S(1)} %reshape.143, f32[4608,144]{1,0:T(8,128)} %gather_fusion.2, f32[4608,144]{1,0:T(8,128)} %gather_fusion.1, f32[4608]{0:T(1024)S(1)} %fusion.27, pred[4608]{0:T(1024)(128)(4,1)S(1)} %compare_and_fusion), kind=kOutput, calls=%fused_computation.49 | convolution fusion | flops 10616832 | bytes 5350464 | tf_op jit(solution)/shard_map/dot_general | solution.py:57
  202.8 35.3 %all-to-all-done.1 = f32[8,36,4608]{2,1,0:T(8,128)} async-done(((f32[8,36,4608]{2,1,0:T(8,128)}), f32[8,36,4608]{2,1,0:T(8,128)}, u32[]{:S(2)}, u32[]{:S(2)}) %all-to-all-start.1) | async-done | bytes 5308448 | tf_op jit(solution)/shard_map/all_to_all | solution.py:59
  238.1 5.6 %reshape.110 = f32[288,4608]{1,0:T(8,128)} reshape(f32[8,36,4608]{2,1,0:T(8,128)} %all-to-all-done.1) | data formatting | bytes 10616832 | tf_op jit(solution)/shard_map/reshape | solution.py:66
  243.8 6.8 %convolution_bitcast_fusion = f32[1,144,4608]{2,1,0:T(8,128)} fusion(f32[288,4608]{1,0:T(8,128)} %reshape.110, s32[288]{0:T(512)S(1)} %convert_element_type.48), kind=kOutput, calls=%fused_computation.9 | convolution fusion | flops 2293277184 | bytes 7963776 | tf_op jit(solution)/shard_map/dot_general | solution.py:66
  (10 shorter events, 0.2 us)
Async XLA Ops:
  7.2 163.8 %copy-start = (f32[1,4608]{1,0:T(1,128)S(1)}, f32[1,4608]{1,0:T(1,128)}, u32[]{:S(2)}) copy-start(f32[1,4608]{1,0:T(1,128)} %param.13) | copy-start | bytes 55300
  7.2 16.0 %copy-start.5 = (s32[1,4608]{1,0:T(1,128)S(1)}, s32[1,4608]{1,0:T(1,128)}, u32[]{:S(2)}) copy-start(s32[1,4608]{1,0:T(1,128)} %param.15) | copy-start | bytes 55300
  7.2 110.4 %all-gather.3.cloned.1.call-start = ((), (), s32[]{:S(2)}) async-start(), calls=%async_computation.2 | async-start | bytes 9732096 | tf_op jit(solution)/shard_map/all_gather | solution.py:28
  11.6 153.6 %all-to-all-start = ((f32[8,1,36]{2,1,0:T(1,128)}), f32[8,1,36]{2,1,0:T(1,128)S(1)}, u32[]{:S(2)}, u32[]{:S(2)}) async-start(f32[8,1,36]{2,1,0:T(1,128)} %convert_element_type.46), calls=%async_computation | async-start | bytes 8192 | tf_op jit(solution)/shard_map/all_to_all | solution.py:41
  23.3 14.2 %copy-start.4 = (bf16[1,144,1024]{2,1,0:T(8,128)(2,1)S(1)}, bf16[1,144,1024]{2,1,0:T(8,128)(2,1)}, u32[]{:S(2)}) copy-start(bf16[1,144,1024]{2,1,0:T(8,128)(2,1)} %param.10) | copy-start | bytes 884740
  37.4 5.7 %copy-start.2 = (f32[1,1024,1024]{2,1,0:T(8,128)S(1)}, f32[1,1024,1024]{2,1,0:T(8,128)}, u32[]{:S(2)}) copy-start(f32[1,1024,1024]{2,1,0:T(8,128)} %param.12) | copy-start | bytes 12582916
  42.3 0.8 copy-start.3
  117.6 7.1 %copy-start.1 = (bf16[1,4608,1024]{2,1,0:T(8,128)(2,1)S(1)}, bf16[1,4608,1024]{2,1,0:T(8,128)(2,1)}, u32[]{:S(2)}) copy-start(bf16[1,4608,1024]{2,1,0:T(8,128)(2,1)} %all-gather.3.cloned.1.call-done) | copy-start | bytes 28311556
  165.3 72.9 %all-to-all-start.1 = ((f32[8,36,4608]{2,1,0:T(8,128)}), f32[8,36,4608]{2,1,0:T(8,128)}, u32[]{:S(2)}, u32[]{:S(2)}) async-start(f32[8,36,4608]{2,1,0:T(8,128)} %reshape.109), calls=%async_computation.1 | async-start | bytes 11796480 | tf_op jit(solution)/shard_map/all_to_all | solution.py:59
Sparse Core Ops, SparseCore 0:
  10.6 106.9 all-gather.2
where the time goes:
time: 258 us; the launch traced here: 257 us
  waiting for transfers between devices  108 us (42%)
  local copies, waits for them, and re-layouts  73.7 us (29%)
  matrix products  46.2 us (18%)
  between operations  14.8 us (6%)
  starting transfers between devices  12.2 us (5%)
  other arithmetic  2.64 us (1%)
    all_gather x1, waiting for transfers between devices, on_device(): panel_all = lax.all_gather(panel_block[0], 'grp', axis=0, tiled=True)  71.8 us
    all_to_all x1, waiting for transfers between devices, on_device(): lax.all_to_all(bucket.reshape(fronts, capacity, col_count), 'front', spli...  35.3 us
    gather x1, local copies, waits for them, and re-layouts, on_device(): kept_weights = jnp.take(weights[0], source) * keep  24.1 us
    gather x1, local copies, waits for them, and re-layouts, on_device(): trail_permuted = jnp.take(trail_rows, source, axis=1)  14.1 us
    gather x1, local copies, waits for them, and re-layouts, on_device(): jnp.take(update, source, axis=1)  14.1 us
    dot_general x3, matrix products, on_device(): lax.dot_general(term, panel_all, (((1,), (1,)), ((), ())), preferred_elem...  13.7 us
    dot_general x1, matrix products, on_device(): bucket = jnp.dot(place.astype(jnp.float32), permuted, precision=HIGHEST)  10.9 us
    dot_general x1, matrix products, on_device(): checksum = jnp.dot(permuted, kept_weights, precision=HIGHEST)  7.47 us
  transfers between devices with their start and end apart: 3, of which 2 were waited for; matrix products, arithmetic and copies ran while one was open for 42% of the time, Pallas kernels for 0%

commit v1 on v0

--- a/solution.py
+++ b/solution.py
@@ -4,6 +4,17 @@
 from jax.sharding import PartitionSpec as P
 
 HIGHEST = lax.Precision.HIGHEST
+
+
+def cut_along(value, dim, size):
+    before, after = (value.shape[:dim], value.shape[dim + 1 :])
+    return jnp.moveaxis(value.reshape(*before, size, -1, *after), dim, 0)
+
+
+def laid_out(blocks, dim):
+    shape = list(blocks.shape[1:])
+    shape[dim] *= blocks.shape[0]
+    return jnp.moveaxis(blocks, 0, dim).reshape(shape)
 
 
 def bf16_terms(x):
@@ -38,7 +49,14 @@
     place = flat_slot[None, :] == jnp.arange(slots, dtype=jnp.int32)[:, None]
     row_tags = jnp.sum(jnp.where(place, row_offset[0][None, :] + 1, 0), axis=1) - 1
     row_tags = row_tags.astype(jnp.float32).reshape(fronts, capacity)
-    received_tags = lax.all_to_all(row_tags, "front", split_axis=0, concat_axis=0, tiled=True)
+    count, index = (lax.axis_size("front"), lax.axis_index("front"))
+    blocks = cut_along(row_tags, 0, count)
+    outs = [blocks[index]]
+    for step in range(1, count):
+        sent = blocks[index ^ step]
+        outs.append(lax.ppermute(sent, "front", [(i, i ^ step) for i in range(count)]))
+    blocks = jnp.stack(outs)[index ^ jnp.arange(count)]
+    received_tags = laid_out(blocks, 0)
     targets = received_tags.reshape(slots).astype(jnp.int32)
     land = (targets[None, :] == rows[:, None]).astype(jnp.float32)
     source = column_source[0]

time: 258 us -> 269 us (1.043)
  waiting for transfers between devices: 108 us -> 116 us
  starting transfers between devices: 12.2 us -> 16.5 us
    all_to_all x1, waiting for transfers between devices: 35.3 us -> 0.01 us  [on_device(): lax.all_to_all(bucket.reshape(fronts, capacity, col_count), 'front', spli...]
    ppermute x0 -> x7, waiting for transfers between devices: none -> 34.6 us  [on_device(): lax.ppermute(sent, 'front', [(i, i ^ step) for i in range(count)])]
    ppermute x0 -> x7, starting transfers between devices: none -> 10.6 us  [on_device(): lax.ppermute(sent, 'front', [(i, i ^ step) for i in range(count)])]
    all_gather x1, waiting for transfers between devices: 71.8 us -> 81.2 us  [on_device(): panel_all = lax.all_gather(panel_block[0], 'grp', axis=0, tiled=True)]
    all_to_all x1 -> x0, starting transfers between devices: 6.45 us -> none  [on_device(): lax.all_to_all(row_tags, 'front', split_axis=0, concat_axis=0, tiled=True)]
    unnamed x13 -> x17, local copies, waits for them, and re-layouts: 5.92 us -> 5.93 us
  transfers between devices with their start and end apart: 3 -> 9, of which waited for: 2 -> 3; matrix products, arithmetic and copies ran while one was open for 42% -> 22% of each run, Pallas kernels for 0% -> 0%
where the time goes in v1:
time: 269 us; the launch traced here: 268 us
  waiting for transfers between devices  116 us (43%)
  local copies, waits for them, and re-layouts  73.7 us (27%)
  matrix products  46.3 us (17%)
  starting transfers between devices  16.5 us (6%)
  between operations  14.9 us (6%)
    all_gather x1, waiting for transfers between devices, on_device(): panel_all = lax.all_gather(panel_block[0], 'grp', axis=0, tiled=True)  81.2 us
    ppermute x7, waiting for transfers between devices, on_device(): lax.ppermute(sent, 'front', [(i, i ^ step) for i in range(count)])  34.6 us
    gather x1, local copies, waits for them, and re-layouts, on_device(): kept_weights = jnp.take(weights[0], source) * keep  24.1 us
    gather x1, local copies, waits for them, and re-layouts, on_device(): trail_permuted = jnp.take(trail_rows, source, axis=1)  14.1 us
    gather x1, local copies, waits for them, and re-layouts, on_device(): jnp.take(update, source, axis=1)  14.1 us
    dot_general x3, matrix products, on_device(): lax.dot_general(term, panel_all, (((1,), (1,)), ((), ())), preferred_elem...  13.7 us
    dot_general x1, matrix products, on_device(): bucket = jnp.dot(place.astype(jnp.float32), permuted, precision=HIGHEST)  10.9 us
    ppermute x7, starting transfers between devices, on_device(): lax.ppermute(sent, 'front', [(i, i ^ step) for i in range(count)])  10.6 us
  transfers between devices with their start and end apart: 9, of which 3 were waited for; matrix products, arithmetic and copies ran while one was open for 22% of the time, Pallas kernels for 0%

profile of v1, /device:TPU:1, one launch (start us, length us, event | category | flops | bytes accessed | tf_op | source)
XLA Modules:
  0.0 268.5 jit_solution(8887571150105876416)
XLA Ops:
  7.2 0.0 copy-start
  7.2 0.0 copy-start.5
  7.2 0.0 all-gather.3.cloned.1.call-start
  7.2 0.7 all-gather.3.cloned.1.call-update
  8.6 5.1 %copy.29 = f32[1,144,4608]{1,2,0:T(8,128)} copy(f32[1,144,4608]{2,1,0:T(8,128)} %param.11) | data formatting | bytes 5308416 | tf_op args[1]
  13.7 0.0 copy-done.5
  13.7 0.0 copy-start.6
  13.8 0.0 copy-start.4
  13.8 14.1 %gather_fusion.2 = f32[4608,144]{1,0:T(8,128)} fusion(f32[144,4608]{0,1:T(8,128)} %bitcast.84, s32[5120]{0:T(1024)S(1)} %pad_clamp_fusion.1), kind=kCustom, calls=%fused_computation.clone | custom fusion | bytes 5326848 | tf_op jit(solution)/shard_map/jit(_take)/gather | solution.py:64
  27.9 0.0 copy-start.2
  27.9 0.1 fusion.27
  28.0 0.0 copy-done.6
  28.0 0.2 convert_reduce_fusion
  28.2 0.0 copy-done.4
  28.2 4.8 %fusion.15 = f32[144,1024]{1,0:T(8,128)S(1)} fusion(f32[1,1024,1024]{2,1,0:T(8,128)} %param.12, bf16[1,144,1024]{2,1,0:T(8,128)(2,1)S(1)} %copy-done.4), kind=kOutput, calls=%fused_computation.17 | convolution fusion | flops 1811939328 | bytes 5079040 | tf_op jit(solution)/shard_map/dot_general | solution.py:41
  33.0 0.0 copy-start.3
  33.0 0.8 copy-done.3
  33.8 0.0 copy-done.2
  33.8 2.6 fusion.13
  36.4 81.2 %all-gather.3.cloned.1.call-done = bf16[1,4608,1024]{2,1,0:T(8,128)(2,1)} async-done(((bf16[1,144,1024]{2,1,0:T(8,128)(2,1)}), bf16[1,4608,1024]{2,1,0:T(8,128)(2,1)}) %all-gather.3.cloned.1.call-update) | async-done | bytes 9437200 | tf_op jit(solution)/shard_map/all_gather | solution.py:39
  117.6 0.0 copy-start.1
  117.6 7.1 %fusion = f32[144,4608]{1,0:T(8,128)S(1)} fusion(bf16[1,4608,1024]{2,1,0:T(8,128)(2,1)} %all-gather.3.cloned.1.call-done, f32[144,1024]{1,0:T(8,128)S(1)} %fusion.13), kind=kOutput, calls=%fused_computation.4 | convolution fusion | flops 1359691776 | bytes 12681216 | tf_op jit(solution)/shard_map/dot_general | solution.py:68
  124.7 0.0 copy-done.1
  124.7 3.3 %fusion.2 = f32[144,4608]{1,0:T(8,128)S(1)} fusion(bf16[1,4608,1024]{2,1,0:T(8,128)(2,1)S(1)} %copy-done.1, f32[144,1024]{1,0:T(8,128)S(1)} %fusion.13), kind=kOutput, calls=%fused_computation.6 | convolution fusion | flops 1359544320 | bytes 12681216 | tf_op jit(solution)/shard_map/dot_general | solution.py:68
  127.9 3.3 %fusion.9 = f32[144,4608]{1,0:T(8,128)S(1)} fusion(f32[144,4608]{1,0:T(8,128)S(1)} %fusion, f32[144,4608]{1,0:T(8,128)S(1)} %fusion.2, bf16[1,4608,1024]{2,1,0:T(8,128)(2,1)S(1)} %copy-done.1, f32[144,1024]{1,0:T(8,128)S(1)} %fusion.13), kind=kOutput, calls=%fused_computation.12 | convolution fusion | flops 1360576512 | bytes 17989632 | tf_op jit(solution)/shard_map/dot_general | solution.py:68
  131.3 3.4 %copy.30 = f32[144,4608]{0,1:T(8,128)} copy(f32[144,4608]{1,0:T(8,128)S(1)} %fusion.9) | data formatting | bytes 5308416 | tf_op jit(solution)/shard_map/add | solution.py:66
  134.7 14.1 %gather_fusion.3 = f32[4608,144]{1,0:T(8,128)} fusion(f32[144,4608]{0,1:T(8,128)} %copy.30, s32[5120]{0:T(1024)S(1)} %pad_clamp_fusion.1), kind=kCustom, calls=%fused_computation.1.clone | custom fusion | bytes 5326848 | tf_op jit(solution)/shard_map/jit(_take)/gather | solution.py:74
  148.8 10.9 %fusion.22 = f32[288,4608]{1,0:T(8,128)} fusion(s32[144]{0:T(256)S(1)} %add_select_fusion, f32[4608,144]{1,0:T(8,128)} %gather_fusion.3, f32[4608,144]{1,0:T(8,128)} %gather_fusion.2, f32[4608]{0:T(1024)S(1)} %fusion.27, pred[4608]{0:T(1024)(128)(4,1)S(1)} %compare_and_fusion), kind=kOutput, calls=%fused_computation.32 | convolution fusion | flops 2295972864 | bytes 10640448 | tf_op jit(solution)/shard_map/dot_general | solution.py:76
  159.6 5.6 %reshape.119 = f32[8,36,4608]{2,1,0:T(8,128)} reshape(f32[288,4608]{1,0:T(8,128)} %fusion.22) | data formatting | bytes 10616832 | tf_op jit(solution)/shard_map/reshape | solution.py:78
  165.2 0.0 copy-start.7
  165.2 5.8 %all-to-all-start = ((f32[8,36,4608]{2,1,0:T(8,128)}), f32[8,36,4608]{2,1,0:T(8,128)}, u32[]{:S(2)}, u32[]{:S(2)}) async-start(f32[8,36,4608]{2,1,0:T(8,128)} %reshape.119), calls=%async_computation | async-start | bytes 11796480 | tf_op jit(solution)/shard_map/all_to_all | solution.py:77
  171.0 0.0 copy-done.7
  171.0 0.1 select_reduce_fusion
  171.2 0.1 convert_element_type.45
  171.3 0.3 collective-permute-start
  171.5 1.6 collective-permute-start.1
  173.1 0.4 collective-permute-start.2
  173.5 2.9 %collective-permute-start.3 = (f32[1,36]{1,0:T(1,128)S(1)}, f32[1,36]{1,0:T(1,128)S(1)}, u32[]{:S(2)}, u32[]{:S(2)}) collective-permute-start(f32[1,36]{1,0:T(1,128)S(1)} %get-tuple-element.7), channel_id=1, source_target_pairs={{0,128},{32,160},{64,192},{96,224},{128,0},{160,32},{192,64},{224,... | collective-permute-start | bytes 440 | tf_op jit(solution)/shard_map/ppermute | solution.py:57
  176.4 0.3 collective-permute-start.4
  176.7 0.0 copy-done
  176.7 0.1 fusion.26
  176.8 24.1 %gather_fusion = f32[4608]{0:T(1024)S(1)} fusion(f32[4608]{0:T(1024)S(1)} %reduce.2, s32[5120]{0:T(1024)S(1)} %pad_clamp_fusion), kind=kCustom, calls=%fused_computation.2 | custom fusion | bytes 55296 | tf_op jit(solution)/shard_map/jit(_take)/gather | solution.py:65
  201.0 0.0 collective-permute-done
  201.0 2.7 %collective-permute-start.5 = (f32[1,36]{1,0:T(1,128)S(1)}, f32[1,36]{1,0:T(1,128)S(1)}, u32[]{:S(2)}, u32[]{:S(2)}) collective-permute-start(f32[1,36]{1,0:T(1,128)S(1)} %get-tuple-element.5), channel_id=1, source_target_pairs={{0,192},{32,224},{64,128},{96,160},{128,64},{160,96},{192,0},{224,... | collective-permute-start | bytes 440 | tf_op jit(solution)/shard_map/ppermute | solution.py:57
  203.7 32.9 %collective-permute-done.1 = f32[1,36]{1,0:T(1,128)S(1)} collective-permute-done((f32[1,36]{1,0:T(1,128)S(1)}, f32[1,36]{1,0:T(1,128)S(1)}, u32[]{:S(2)}, u32[]{:S(2)}) %collective-permute-start.1) | collective-permute-done | bytes 176 | tf_op jit(solution)/shard_map/ppermute | solution.py:57
  236.7 2.5 collective-permute-start.6
  239.1 0.0 collective-permute-done.2
  239.1 0.0 collective-permute-done.3
  239.2 0.0 collective-permute-done.4
  239.2 0.0 collective-permute-done.5
  239.2 1.7 collective-permute-done.6
  240.9 0.6 gather_fusion.1
  241.4 0.1 convert_element_type.47
  241.5 7.7 %fusion.38 = f32[1,144]{1,0:T(1,128)} fusion(f32[4608,1]{0,1:T(1,128)S(1)} %reshape.165, f32[4608,144]{1,0:T(8,128)} %gather_fusion.3, f32[4608,144]{1,0:T(8,128)} %gather_fusion.2, f32[4608]{0:T(1024)S(1)} %fusion.27, pred[4608]{0:T(1024)(128)(4,1)S(1)} %compare_and_fusion), kind=kOutput, calls=%fused_computation.67 | convolution fusion | flops 10616832 | bytes 5350464 | tf_op jit(solution)/shard_map/dot_general | solution.py:75
  249.2 0.0 all-to-all-done
  249.2 5.6 %reshape.120 = f32[288,4608]{1,0:T(8,128)} reshape(f32[8,36,4608]{2,1,0:T(8,128)} %all-to-all-done) | data formatting | bytes 10616832 | tf_op jit(solution)/shard_map/reshape | solution.py:84
  254.8 6.8 %convolution_bitcast_fusion = f32[1,144,4608]{2,1,0:T(8,128)} fusion(f32[288,4608]{1,0:T(8,128)} %reshape.120, s32[288]{0:T(512)S(1)} %convert_element_type.47), kind=kOutput, calls=%fused_computation.10 | convolution fusion | flops 2293277184 | bytes 7963776 | tf_op jit(solution)/shard_map/dot_general | solution.py:84
  (17 shorter events, 0.2 us)
Async XLA Ops:
  7.2 169.5 %copy-start = (f32[1,4608]{1,0:T(1,128)S(1)}, f32[1,4608]{1,0:T(1,128)}, u32[]{:S(2)}) copy-start(f32[1,4608]{1,0:T(1,128)} %param.13) | copy-start | bytes 55300
  7.2 6.5 %copy-start.5 = (s32[1,4608]{1,0:T(1,128)S(1)}, s32[1,4608]{1,0:T(1,128)}, u32[]{:S(2)}) copy-start(s32[1,4608]{1,0:T(1,128)} %param.15) | copy-start | bytes 55300
  7.2 110.4 %all-gather.3.cloned.1.call-start = ((), (), s32[]{:S(2)}) async-start(), calls=%async_computation.1 | async-start | bytes 9732096 | tf_op jit(solution)/shard_map/all_gather | solution.py:39
  13.7 14.2 %copy-start.6 = (s32[1,144,1]{1,2,0:T(1,128)S(1)}, s32[1,144,1]{1,2,0:T(1,128)}, u32[]{:S(2)}) copy-start(s32[1,144,1]{1,2,0:T(1,128)} %param.16) | copy-start | bytes 1732
  13.8 14.5 %copy-start.4 = (bf16[1,144,1024]{2,1,0:T(8,128)(2,1)S(1)}, bf16[1,144,1024]{2,1,0:T(8,128)(2,1)}, u32[]{:S(2)}) copy-start(bf16[1,144,1024]{2,1,0:T(8,128)(2,1)} %param.10) | copy-start | bytes 884740
  27.9 5.9 %copy-start.2 = (f32[1,1024,1024]{2,1,0:T(8,128)S(1)}, f32[1,1024,1024]{2,1,0:T(8,128)}, u32[]{:S(2)}) copy-start(f32[1,1024,1024]{2,1,0:T(8,128)} %param.12) | copy-start | bytes 12582916
  33.0 0.8 copy-start.3
  117.6 7.1 %copy-start.1 = (bf16[1,4608,1024]{2,1,0:T(8,128)(2,1)S(1)}, bf16[1,4608,1024]{2,1,0:T(8,128)(2,1)}, u32[]{:S(2)}) copy-start(bf16[1,4608,1024]{2,1,0:T(8,128)(2,1)} %all-gather.3.cloned.1.call-done) | copy-start | bytes 28311556
  165.2 5.8 %copy-start.7 = (s32[1,144]{1,0:T(1,128)S(1)}, s32[1,144]{1,0:T(1,128)}, u32[]{:S(2)}) copy-start(s32[1,144]{1,0:T(1,128)} %param.17) | copy-start | bytes 1732
  165.2 84.0 %all-to-all-start = ((f32[8,36,4608]{2,1,0:T(8,128)}), f32[8,36,4608]{2,1,0:T(8,128)}, u32[]{:S(2)}, u32[]{:S(2)}) async-start(f32[8,36,4608]{2,1,0:T(8,128)} %reshape.119), calls=%async_computation | async-start | bytes 11796480 | tf_op jit(solution)/shard_map/all_to_all | solution.py:77
  171.3 29.7 %collective-permute-start = (f32[1,36]{1,0:T(1,128)S(1)}, f32[1,36]{1,0:T(1,128)S(1)}, u32[]{:S(2)}, u32[]{:S(2)}) collective-permute-start(f32[1,36]{1,0:T(1,128)S(1)} %get-tuple-element.10), channel_id=1, source_target_pairs={{0,32},{32,0},{64,96},{96,64},{128,160},{160,128},{192,224},{224,1... | collective-permute-start | bytes 440 | tf_op jit(solution)/shard_map/ppermute | solution.py:57
  171.5 65.1 %collective-permute-start.1 = (f32[1,36]{1,0:T(1,128)S(1)}, f32[1,36]{1,0:T(1,128)S(1)}, u32[]{:S(2)}, u32[]{:S(2)}) collective-permute-start(f32[1,36]{1,0:T(1,128)S(1)} %get-tuple-element.9), channel_id=1, source_target_pairs={{0,64},{32,96},{64,0},{96,32},{128,192},{160,224},{192,128},{224,1... | collective-permute-start | bytes 440 | tf_op jit(solution)/shard_map/ppermute | solution.py:57
  173.1 66.0 %collective-permute-start.2 = (f32[1,36]{1,0:T(1,128)S(1)}, f32[1,36]{1,0:T(1,128)S(1)}, u32[]{:S(2)}, u32[]{:S(2)}) collective-permute-start(f32[1,36]{1,0:T(1,128)S(1)} %get-tuple-element.8), channel_id=1, source_target_pairs={{0,96},{32,64},{64,32},{96,0},{128,224},{160,192},{192,160},{224,1... | collective-permute-start | bytes 440 | tf_op jit(solution)/shard_map/ppermute | solution.py:57
  173.5 65.7 %collective-permute-start.3 = (f32[1,36]{1,0:T(1,128)S(1)}, f32[1,36]{1,0:T(1,128)S(1)}, u32[]{:S(2)}, u32[]{:S(2)}) collective-permute-start(f32[1,36]{1,0:T(1,128)S(1)} %get-tuple-element.7), channel_id=1, source_target_pairs={{0,128},{32,160},{64,192},{96,224},{128,0},{160,32},{192,64},{224,... | collective-permute-start | bytes 440 | tf_op jit(solution)/shard_map/ppermute | solution.py:57
  176.4 62.7 %collective-permute-start.4 = (f32[1,36]{1,0:T(1,128)S(1)}, f32[1,36]{1,0:T(1,128)S(1)}, u32[]{:S(2)}, u32[]{:S(2)}) collective-permute-start(f32[1,36]{1,0:T(1,128)S(1)} %get-tuple-element.6), channel_id=1, source_target_pairs={{0,160},{32,128},{64,224},{96,192},{128,32},{160,0},{192,96},{224,... | collective-permute-start | bytes 440 | tf_op jit(solution)/shard_map/ppermute | solution.py:57
  201.0 38.2 %collective-permute-start.5 = (f32[1,36]{1,0:T(1,128)S(1)}, f32[1,36]{1,0:T(1,128)S(1)}, u32[]{:S(2)}, u32[]{:S(2)}) collective-permute-start(f32[1,36]{1,0:T(1,128)S(1)} %get-tuple-element.5), channel_id=1, source_target_pairs={{0,192},{32,224},{64,128},{96,160},{128,64},{160,96},{192,0},{224,... | collective-permute-start | bytes 440 | tf_op jit(solution)/shard_map/ppermute | solution.py:57
  236.7 4.2 %collective-permute-start.6 = (f32[1,36]{1,0:T(1,128)S(1)}, f32[1,36]{1,0:T(1,128)S(1)}, u32[]{:S(2)}, u32[]{:S(2)}) collective-permute-start(f32[1,36]{1,0:T(1,128)S(1)} %get-tuple-element.4), channel_id=1, source_target_pairs={{0,224},{32,192},{64,160},{96,128},{128,96},{160,64},{192,32},{224... | collective-permute-start | bytes 440 | tf_op jit(solution)/shard_map/ppermute | solution.py:57
Sparse Core Ops, SparseCore 0:
  10.6 106.9 all-gather.2
